TPU v7x, 256 devices: a whole 4x4x8 slice. The times are simulated.
256 devices in a mesh: seq: 32 (over y, z), head: 4 (over x), dp: 2 (over core).
Axes of the slice: x: 4, y: 4, z: 8, core: 2. Of those that a mesh axis runs over, the one named last changes fastest.
Arguments:
- tokens: bfloat16 [65536, 2048], P(('dp', 'seq', 'head')), parts along dimension 0, may hold values from -6 to 6
- qkv_weight: bfloat16 [2048, 3, 2048], P(None, None, 'head'), may hold values from -0.125 to 0.125
- out_weight: bfloat16 [2048, 2048], P('head'), may hold values from -0.125 to 0.125
- prefix_state: float32 [32, 128, 128], P(('dp', 'head')), parts along dimension 0, may hold values from -1536 to 1536
Outputs:
- layer_out: bfloat16 [65536, 2048], P(('dp', 'seq', 'head')), parts along dimension 0
There are 2 independent parts, one for each index of `dp`. A program takes and returns all parts, laid end to end along the dimension named above; an argument that names none is the same for every part. Nothing has to cross between parts.
All inputs are finite; a program needn't handle non-finite values.
Results may differ from a plain program's by a relative error of at most 0.014.
Values may be sent and summed in bfloat16 or wider, within the bound.
A program may use at most 64 MiB of HBM per device.

v0:
```python
import jax
import jax.numpy as jnp
from jax import lax
from jax.sharding import PartitionSpec as P


def on_device(tokens, qkv_weight, out_weight, prefix_state):
    model_width = qkv_weight.shape[0]
    head_size = prefix_state.shape[1]
    group_heads = prefix_state.shape[0]
    group_width = group_heads * head_size
    flat = qkv_weight.reshape(model_width, 3 * group_width)
    projected = jnp.dot(
        lax.all_gather(tokens, "head", axis=0, tiled=True), flat, preferred_element_type=jnp.float32
    ).astype(jnp.bfloat16)
    length = projected.shape[0]
    query = projected[:, :group_width].reshape(length, group_heads, head_size)
    keys = projected[:, group_width : 2 * group_width].reshape(length, group_heads, head_size)
    values = projected[:, 2 * group_width :].reshape(length, group_heads, head_size)
    local_state = jnp.einsum("thd,the->hde", keys, values, preferred_element_type=jnp.float32)
    my_block = lax.axis_index("seq")
    piece = lax.all_gather(
        local_state[None].astype(jnp.bfloat16), "seq", axis=0, tiled=True
    ).astype(jnp.float32)
    count = piece.shape[0]
    keep = (jnp.arange(count) < my_block).astype(jnp.float32)
    carried = prefix_state + jnp.sum(piece * keep[:, None, None, None], axis=0)
    carried_low = carried.astype(jnp.bfloat16)
    block = min(512, length)
    pieces = []
    for number in range(length // block):
        lower = number * block
        upper = lower + block
        block_q = query[lower:upper]
        scores = jnp.einsum(
            "shd,thd->hst", block_q, keys[:upper], preferred_element_type=jnp.float32
        )
        causal = (lower + jnp.arange(block))[:, None] >= jnp.arange(upper)[None, :]
        weights = jnp.where(causal[None], scores, 0.0).astype(jnp.bfloat16)
        mixed = jnp.einsum(
            "hst,thd->shd", weights, values[:upper], preferred_element_type=jnp.float32
        )
        mixed = mixed + jnp.einsum(
            "shd,hde->she", block_q, carried_low, preferred_element_type=jnp.float32
        )
        factor = lax.rsqrt(jnp.mean(mixed * mixed, axis=-1, keepdims=True) + 1e-06)
        pieces.append((mixed * factor).astype(jnp.bfloat16).reshape(block, group_width))
    normed = jnp.concatenate(pieces, axis=0)
    summed = lax.psum_scatter(
        jnp.dot(normed, out_weight, preferred_element_type=jnp.float32).astype(jnp.bfloat16),
        "head",
        scatter_dimension=0,
        tiled=True,
    ).astype(jnp.float32)
    return (tokens.astype(jnp.float32) + summed).astype(jnp.bfloat16)


def solution(mesh):
    return jax.shard_map(
        on_device,
        mesh=mesh,
        in_specs=(
            P(("dp", "seq", "head"), None),
            P(None, None, "head"),
            P("head", None),
            P(("dp", "head"), None, None),
        ),
        out_specs=P(("dp", "seq", "head"), None),
        check_vma=False,
    )
```

profile of v0, /device:TPU:1, one launch (start us, length us, event | category | flops | bytes accessed | tf_op | source)
XLA Modules:
  0.0 235.1 jit_solution(14859158136180378359)
XLA Ops:
  6.5 0.0 copy-start
  6.5 0.0 all-gather.4.cloned.1.call-start
  6.5 0.7 all-gather.4.cloned.1.call-update
  7.3 0.0 all-gather.6.cloned.1.call-start
  7.3 8.9 %copy.22 = bf16[2048,3,512]{0,2,1:T(8,128)(2,1)} copy(bf16[2048,3,512]{2,0,1:T(8,128)(2,1)} %param.5) | data formatting | bytes 12582912 | tf_op args[1]
  16.2 47.6 %all-gather.4.cloned.1.call-done = bf16[1024,2048]{1,0:T(8,128)(2,1)} async-done(((bf16[256,2048]{1,0:T(8,128)(2,1)}), bf16[1024,2048]{1,0:T(8,128)(2,1)}) %all-gather.4.cloned.1.call-update) | async-done | bytes 4194320 | tf_op jit(solution)/shard_map/all_gather | solution.py:14
  63.8 10.1 %convolution_convert_fusion = bf16[1024,1536]{1,0:T(8,128)(2,1)S(1)} fusion(bf16[1024,2048]{1,0:T(8,128)(2,1)} %all-gather.4.cloned.1.call-done, bf16[2048,1536]{0,1:T(8,128)(2,1)} %bitcast.55), kind=kOutput, calls=%fused_computation.7 | convolution fusion | flops 6444023808 | bytes 13631488 | tf_op jit(solution)/shard_map/dot_general | solution.py:13
  73.9 0.0 copy-start.1
  73.9 1.7 copy-done.1
  75.5 1.2 slice_bitcast_fusion
  76.7 1.4 copy.38
  78.1 2.7 %convolution_convert_fusion.2 = bf16[4,128,128]{2,1,0:T(8,128)(2,1)} fusion(bf16[1024,4,128]{0,2,1:T(8,128)(2,1)} %bitcast.57, bf16[128,4,8,128]{3,2,1,0:T(8,128)(2,1)} %get-tuple-element.9), kind=kOutput, calls=%fused_computation.17 | convolution fusion | flops 134283264 | bytes 2228224 | tf_op jit(solution)/shard_map/thd,the->hde/dot_general | solution.py:20
  80.8 0.0 all-gather.6.cloned.1.call-update
  80.8 0.2 reduce-scatter.2.cloned.1.call-start
  81.1 0.8 iota_compare_fusion.1
  81.9 1.2 iota_compare_fusion
  83.0 3.0 %slice_bitcast_fusion.2 = (bf16[64,4,8,128]{3,2,1,0:T(8,128)(2,1)}, bf16[64,4,8,128]{3,2,1,0:T(8,128)(2,1)}, bf16[64,4,8,128]{3,2,1,0:T(8,128)(2,1)S(1)}, bf16[512,512]{1,0:T(8,128)(2,1)S(1)}) fusion(bf16[1024,1536]{1,0:T(8,128)(2,1)} %copy-done.1), kind=kLoop, calls=%fused_computation.39 | loop fusion | bytes 4194304
  86.0 1.0 copy.37
  87.0 5.4 %fusion.1 = f32[4,128,512]{2,1,0:T(8,128)} fusion(bf16[1024,4,128]{0,2,1:T(8,128)(2,1)} %bitcast.58, pred[512,1024]{1,0:T(8,128)(4,1)} %iota_compare_fusion, bf16[128,4,8,128]{3,2,1,0:T(8,128)(2,1)} %get-tuple-element.9, bf16[64,4,8,128]{3,2,1,0:T(8,128)(2,1)} %get-tuple-element.6), kind=kOutput, calls=%fused_computation.3 | convolution fusion | flops 1077936128 | bytes 4194304 | tf_op jit(solution)/shard_map/hst,thd->shd/dot_general | solution.py:40
  92.4 68.1 %all-gather.6.cloned.1.call-done = bf16[128,128,128]{2,1,0:T(8,128)(2,1)} async-done(((bf16[4,128,128]{2,1,0:T(8,128)(2,1)}), bf16[128,128,128]{2,1,0:T(8,128)(2,1)}) %all-gather.6.cloned.1.call-update) | async-done | bytes 4194320 | tf_op jit(solution)/shard_map/all_gather | solution.py:22
  160.5 3.2 %fusion = f32[4,128,128]{2,1,0:T(8,128)S(1)} fusion(bf16[32,4,128,128]{3,2,1,0:T(8,128)(2,1)} %bitcast.56, f32[32]{0:T(128)S(1)} %compare_convert_fusion), kind=kLoop, calls=%fused_computation.1 | loop fusion | flops 6225920 | bytes 4456576 | tf_op jit(solution)/shard_map/reduce_sum | solution.py:27
  163.7 0.0 copy-done.4
  163.8 0.0 copy-start.3
  163.8 1.3 fusion.26
  165.1 3.9 %multiply_reduce_fusion.1 = (f32[512,4]{0,1:T(4,128)S(1)}, f32[512,4,128]{0,2,1:T(8,128)}) fusion(f32[4,128,512]{2,1,0:T(8,128)} %fusion.26, bf16[512,4,128]{0,2,1:T(8,128)(2,1)} %bitcast.61, pred[512,512]{1,0:T(8,128)(4,1)} %iota_compare_fusion.1, bf16[64,4,8,128]{3,2,1,0:T(8,128)(2,1)} %get-tuple-element.5, bf16[64,4,8,128]{3,2,1,0:T(8,128)(2,1)S(1)} %get-tuple-element.7), kind=kOutput, calls=%fused_computation.27 | convolution fusion | flops 539752448 | bytes 3940352 | tf_op jit(solution)/shard_map/hst,thd->shd/dot_general | solution.py:40
  169.1 1.6 multiply_reduce_fusion
  170.7 1.4 multiply_convert_fusion.1
  172.1 0.1 multiply_convert_fusion
  172.2 4.3 %convolution_convert_fusion.1 = bf16[1024,2048]{1,0:T(8,128)(2,1)} fusion(bf16[512,2048]{1,0:T(8,128)(2,1)S(1)} %copy-done, bf16[512,512]{0,1:T(8,128)(2,1)S(1)} %bitcast.60, bf16[512,512]{0,1:T(8,128)(2,1)S(1)} %bitcast.59), kind=kOutput, calls=%fused_computation.8 | convolution fusion | flops 2151677952 | bytes 7340032 | tf_op jit(solution)/shard_map/dot_general | solution.py:50
  176.5 0.0 reduce-scatter.2.cloned.1.call-update
  176.6 49.4 %reduce-scatter.2.cloned.1.call-done = bf16[256,2048]{1,0:T(8,128)(2,1)} async-done(((bf16[1024,2048]{1,0:T(8,128)(2,1)}), bf16[256,2048]{1,0:T(8,128)(2,1)}) %reduce-scatter.2.cloned.1.call-update) | async-done | bytes 1048592 | tf_op jit(solution)/shard_map/reduce_scatter | solution.py:49
  226.0 2.6 %add_convert_fusion = bf16[256,2048]{1,0:T(8,128)(2,1)} fusion(bf16[256,2048]{1,0:T(8,128)(2,1)} %reduce-scatter.2.cloned.1.call-done, bf16[256,2048]{1,0:T(8,128)(2,1)S(1)} %copy-done.2), kind=kLoop, calls=%fused_computation.10 | loop fusion | flops 2097152 | bytes 3145728 | tf_op jit(solution)/shard_map/convert_element_type | solution.py:55
  (10 shorter events, 0.1 us)
Async XLA Ops:
  6.5 165.7 %copy-start = (bf16[512,2048]{1,0:T(8,128)(2,1)S(1)}, bf16[512,2048]{1,0:T(8,128)(2,1)}, u32[]{:S(2)}) copy-start(bf16[512,2048]{1,0:T(8,128)(2,1)} %param.6) | copy-start | bytes 6291460
  6.5 57.3 %all-gather.4.cloned.1.call-start = ((), (), s32[]{:S(2)}) async-start(), calls=%async_computation.1 | async-start | bytes 5242880 | tf_op jit(solution)/shard_map/all_gather | solution.py:14
  7.3 153.3 %all-gather.6.cloned.1.call-start = ((), (), s32[]{:S(2)}) async-start(), calls=%async_computation.3 | async-start | bytes 4325376 | tf_op jit(solution)/shard_map/all_gather | solution.py:22
  73.9 1.7 copy-start.1
  80.8 145.1 %reduce-scatter.2.cloned.1.call-start = ((), (), s32[]{:S(2)}) async-start(), calls=%async_computation.2 | async-start | bytes 5242880 | tf_op jit(solution)/shard_map/reduce_scatter | solution.py:49
  92.4 71.3 %copy-start.4 = (f32[4,128,128]{2,1,0:T(8,128)S(1)}, f32[4,128,128]{2,1,0:T(8,128)}, u32[]{:S(2)}) copy-start(f32[4,128,128]{2,1,0:T(8,128)} %param.7) | copy-start | bytes 786436
  163.8 5.3 %copy-start.3 = (bf16[64,4,8,128]{3,2,1,0:T(8,128)(2,1)S(1)}, bf16[64,4,8,128]{3,2,1,0:T(8,128)(2,1)}, u32[]{:S(2)}) copy-start(bf16[64,4,8,128]{3,2,1,0:T(8,128)(2,1)} %get-tuple-element.6) | copy-start | bytes 1572868
  176.5 49.5 %copy-start.2 = (bf16[256,2048]{1,0:T(8,128)(2,1)S(1)}, bf16[256,2048]{1,0:T(8,128)(2,1)}, u32[]{:S(2)}) copy-start(bf16[256,2048]{1,0:T(8,128)(2,1)} %param.4) | copy-start | bytes 3145732
Sparse Core Ops, SparseCore 0:
  9.2 54.5 all-gather.3
  81.0 79.5 all-gather.5
  176.7 49.2 reduce-scatter.1
where the time goes:
time: 236 us; the launch traced here: 235 us
  waiting for transfers between devices  166 us (70%)
  matrix products  29.4 us (12%)
  local copies, waits for them, and re-layouts  17.1 us (7%)
  between operations  13.2 us (6%)
  other arithmetic  9.26 us (4%)
    all_gather x1, waiting for transfers between devices, on_device(): lax.all_gather(local_state[None].astype(jnp.bfloat16), 'seq', axis=0, til...  68.1 us
    reduce_scatter x1, waiting for transfers between devices, on_device(): lax.psum_scatter(jnp.dot(normed, out_weight, preferred_element_type=jnp.f...  49.4 us
    all_gather x1, waiting for transfers between devices, on_device(): lax.all_gather(tokens, 'head', axis=0, tiled=True)  47.6 us
    unnamed x13, local copies, waits for them, and re-layouts  14.7 us
    dot_general x1, matrix products, on_device(): jnp.dot(lax.all_gather(tokens, 'head', axis=0, tiled=True), flat, preferr...  10.1 us
    dot_general x2, matrix products, on_device(): jnp.einsum('hst,thd->shd', weights, values[:upper], preferred_element_typ...  9.34 us
  transfers between devices with their start and end apart: 3, of which 3 were waited for; matrix products, arithmetic and copies ran while one was open for 9% of the time, Pallas kernels for 0%

commit v1 on v0

--- a/solution.py
+++ b/solution.py
@@ -2,6 +2,11 @@
 import jax.numpy as jnp
 from jax import lax
 from jax.sharding import PartitionSpec as P
+
+
+def exchange_gather(x, axis, along):
+    sent = jnp.stack([x] * lax.axis_size(axis))
+    return jnp.concatenate(lax.all_to_all(sent, axis, 0, 0), axis=along)
 
 
 def on_device(tokens, qkv_weight, out_weight, prefix_state):
@@ -19,9 +24,7 @@
     values = projected[:, 2 * group_width :].reshape(length, group_heads, head_size)
     local_state = jnp.einsum("thd,the->hde", keys, values, preferred_element_type=jnp.float32)
     my_block = lax.axis_index("seq")
-    piece = lax.all_gather(
-        local_state[None].astype(jnp.bfloat16), "seq", axis=0, tiled=True
-    ).astype(jnp.float32)
+    piece = exchange_gather(local_state[None].astype(jnp.bfloat16), "seq", 0).astype(jnp.float32)
     count = piece.shape[0]
     keep = (jnp.arange(count) < my_block).astype(jnp.float32)
     carried = prefix_state + jnp.sum(piece * keep[:, None, None, None], axis=0)

time: 236 us -> 260 us (1.10)
  waiting for transfers between devices: 166 us -> 180 us
  starting transfers between devices: 0.26 us -> 9.93 us
  local copies, waits for them, and re-layouts: 17.1 us -> 20.1 us
    all_to_all x0 -> x1, waiting for transfers between devices: none -> 82 us  [exchange_gather(): return jnp.concatenate(lax.all_to_all(sent, axis, 0, 0), axis=along)]
    all_gather x1 -> x0, waiting for transfers between devices: 68.1 us -> none  [on_device(): lax.all_gather(local_state[None].astype(jnp.bfloat16), 'seq', axis=0, til...]
    all_to_all x0 -> x1, starting transfers between devices: none -> 9.7 us  [exchange_gather(): return jnp.concatenate(lax.all_to_all(sent, axis, 0, 0), axis=along)]
    another operation x0 -> x1, local copies, waits for them, and re-layouts: none -> 3.03 us  [exchange_gather(): sent = jnp.stack([x] * lax.axis_size(axis))]
    unnamed x13 -> x19, local copies, waits for them, and re-layouts: 14.7 us -> 14.8 us
  transfers between devices with their start and end apart: 3 -> 3, of which waited for: 3 -> 3; matrix products, arithmetic and copies ran while one was open for 9% -> 7% of each run, Pallas kernels for 0% -> 0%
where the time goes in v1:
time: 260 us
  waiting for transfers between devices  180 us (69%)
  matrix products  27.5 us (11%)
  local copies, waits for them, and re-layouts  20.1 us (8%)
  between operations  13.5 us (5%)
  starting transfers between devices  9.93 us (4%)
  other arithmetic  8.72 us (3%)
    all_to_all x1, waiting for transfers between devices, exchange_gather(): return jnp.concatenate(lax.all_to_all(sent, axis, 0, 0), axis=along)  82 us
    reduce_scatter x1, waiting for transfers between devices, on_device(): lax.psum_scatter(jnp.dot(normed, out_weight, preferred_element_type=jnp.f...  49.8 us
    all_gather x1, waiting for transfers between devices, on_device(): lax.all_gather(tokens, 'head', axis=0, tiled=True)  47.6 us
    unnamed x19, local copies, waits for them, and re-layouts  14.8 us
    dot_general x1, matrix products, on_device(): jnp.dot(lax.all_gather(tokens, 'head', axis=0, tiled=True), flat, preferr...  10.1 us
    all_to_all x1, starting transfers between devices, exchange_gather(): return jnp.concatenate(lax.all_to_all(sent, axis, 0, 0), axis=along)  9.7 us
    dot_general x2, matrix products, on_device(): jnp.einsum('hst,thd->shd', weights, values[:upper], preferred_element_typ...  9.34 us
  transfers between devices with their start and end apart: 3, of which 3 were waited for; matrix products, arithmetic and copies ran while one was open for 7% of the time, Pallas kernels for 0%

profile of v1, /device:TPU:1, one launch (start us, length us, event | category | flops | bytes accessed | tf_op | source)
XLA Modules:
  0.0 259.9 jit_solution(15386912755986424045)
XLA Ops:
  6.5 0.0 copy-start
  6.5 0.7 all-gather.2.cloned.1.call-update
  7.3 8.9 %copy.35 = bf16[2048,3,512]{0,2,1:T(8,128)(2,1)} copy(bf16[2048,3,512]{2,0,1:T(8,128)(2,1)} %param.5) | data formatting | bytes 12582912 | tf_op args[1]
  16.2 47.6 %all-gather.2.cloned.1.call-done = bf16[1024,2048]{1,0:T(8,128)(2,1)} async-done(((bf16[256,2048]{1,0:T(8,128)(2,1)}), bf16[1024,2048]{1,0:T(8,128)(2,1)}) %all-gather.2.cloned.1.call-update) | async-done | bytes 4194320 | tf_op jit(solution)/shard_map/all_gather | solution.py:19
  63.8 10.1 %convolution_convert_fusion = bf16[1024,1536]{1,0:T(8,128)(2,1)S(1)} fusion(bf16[1024,2048]{1,0:T(8,128)(2,1)} %all-gather.2.cloned.1.call-done, bf16[2048,1536]{0,1:T(8,128)(2,1)} %bitcast.56), kind=kOutput, calls=%fused_computation.7 | convolution fusion | flops 6444023808 | bytes 13631488 | tf_op jit(solution)/shard_map/dot_general | solution.py:18
  73.9 1.7 copy-done.1
  75.6 1.2 slice_bitcast_fusion
  76.8 1.3 copy.51
  78.1 2.1 convolution_convert_fusion.2
  80.2 3.0 %stack.2 = bf16[32,1,4,128,128]{4,3,2,1,0:T(8,128)(2,1)} broadcast(bf16[4,128,128]{2,1,0:T(8,128)(2,1)S(1)} %convolution_convert_fusion.2), dimensions={2,3,4} | broadcast | bytes 4325376 | tf_op jit(solution)/shard_map/stack | solution.py:8
  83.2 9.7 %all-to-all-start = ((bf16[32,1,4,128,128]{4,3,2,1,0:T(8,128)(2,1)}), bf16[32,1,4,128,128]{4,3,2,1,0:T(8,128)(2,1)}, u32[]{:S(2)}, u32[]{:S(2)}) async-start(bf16[32,1,4,128,128]{4,3,2,1,0:T(8,128)(2,1)} %stack.2), calls=%async_computation | async-start | bytes 8388608 | tf_op jit(solution)/shard_map/all_to_all | solution.py:9
  92.9 0.2 reduce-scatter.2.cloned.1.call-start
  93.2 0.1 iota_compare_fusion.1
  93.3 1.2 iota_compare_fusion
  94.4 2.9 %slice_bitcast_fusion.2 = (bf16[64,4,8,128]{3,2,1,0:T(8,128)(2,1)}, bf16[64,4,8,128]{3,2,1,0:T(8,128)(2,1)S(1)}, bf16[64,4,8,128]{3,2,1,0:T(8,128)(2,1)}, bf16[512,512]{1,0:T(8,128)(2,1)S(1)}) fusion(bf16[1024,1536]{1,0:T(8,128)(2,1)} %copy-done.1), kind=kLoop, calls=%fused_computation.39 | loop fusion | bytes 4194304
  97.4 1.0 copy.50
  98.4 5.3 %fusion.1 = f32[4,128,512]{2,1,0:T(8,128)} fusion(bf16[1024,4,128]{0,2,1:T(8,128)(2,1)} %bitcast.58, pred[512,1024]{1,0:T(8,128)(4,1)} %iota_compare_fusion, bf16[128,4,8,128]{3,2,1,0:T(8,128)(2,1)} %get-tuple-element.9, bf16[64,4,8,128]{3,2,1,0:T(8,128)(2,1)S(1)} %get-tuple-element.6), kind=kOutput, calls=%fused_computation.3 | convolution fusion | flops 1077936128 | bytes 4194304 | tf_op jit(solution)/shard_map/hst,thd->shd/dot_general | solution.py:43
  103.7 82.0 %all-to-all-done = bf16[32,1,4,128,128]{4,3,2,1,0:T(8,128)(2,1)} async-done(((bf16[32,1,4,128,128]{4,3,2,1,0:T(8,128)(2,1)}), bf16[32,1,4,128,128]{4,3,2,1,0:T(8,128)(2,1)}, u32[]{:S(2)}, u32[]{:S(2)}) %all-to-all-start) | async-done | bytes 4194336 | tf_op jit(solution)/shard_map/all_to_all | solution.py:9
  185.7 3.4 %fusion = f32[4,128,128]{2,1,0:T(8,128)S(1)} fusion(bf16[32,1,4,128,128]{4,3,2,1,0:T(8,128)(2,1)} %all-to-all-done, f32[32]{0:T(128)S(1)} %compare_convert_fusion), kind=kLoop, calls=%fused_computation.1 | loop fusion | flops 6225920 | bytes 4456576 | tf_op jit(solution)/shard_map/reduce_sum | solution.py:30
  189.1 0.0 copy-done.5
  189.1 0.0 copy-done.6
  189.1 0.4 multiply_reduce_fusion
  189.5 0.0 copy-done.3
  189.5 1.3 fusion.26
  190.8 4.0 %multiply_reduce_fusion.1 = (f32[512,4]{0,1:T(4,128)S(1)}, f32[512,4,128]{0,2,1:T(8,128)}) fusion(f32[4,128,512]{2,1,0:T(8,128)} %fusion.26, bf16[512,4,128]{0,2,1:T(8,128)(2,1)} %bitcast.61, pred[512,512]{1,0:T(8,128)(4,1)S(1)} %iota_compare_fusion.1, bf16[64,4,8,128]{3,2,1,0:T(8,128)(2,1)} %get-tuple-element.5, bf16[64,4,8,128]{3,2,1,0:T(8,128)(2,1)} %get-tuple-element.7), kind=kOutput, calls=%fused_computation.27 | convolution fusion | flops 539752448 | bytes 3940352 | tf_op jit(solution)/shard_map/hst,thd->shd/dot_general | solution.py:43
  194.9 0.1 multiply_convert_fusion
  195.0 1.4 multiply_convert_fusion.1
  196.4 4.3 %convolution_convert_fusion.1 = bf16[1024,2048]{1,0:T(8,128)(2,1)} fusion(bf16[512,2048]{1,0:T(8,128)(2,1)S(1)} %copy-done, bf16[512,512]{0,1:T(8,128)(2,1)S(1)} %bitcast.59, bf16[512,512]{0,1:T(8,128)(2,1)S(1)} %bitcast.60), kind=kOutput, calls=%fused_computation.8 | convolution fusion | flops 2151677952 | bytes 7340032 | tf_op jit(solution)/shard_map/dot_general | solution.py:53
  200.7 0.0 reduce-scatter.2.cloned.1.call-update
  200.7 49.8 %reduce-scatter.2.cloned.1.call-done = bf16[256,2048]{1,0:T(8,128)(2,1)} async-done(((bf16[1024,2048]{1,0:T(8,128)(2,1)}), bf16[256,2048]{1,0:T(8,128)(2,1)}) %reduce-scatter.2.cloned.1.call-update) | async-done | bytes 1048592 | tf_op jit(solution)/shard_map/reduce_scatter | solution.py:52
  250.5 0.0 copy-done.2
  250.5 2.6 add_convert_fusion
  (16 shorter events, 0.1 us)
Async XLA Ops:
  6.5 189.8 %copy-start = (bf16[512,2048]{1,0:T(8,128)(2,1)S(1)}, bf16[512,2048]{1,0:T(8,128)(2,1)}, u32[]{:S(2)}) copy-start(bf16[512,2048]{1,0:T(8,128)(2,1)} %param.6) | copy-start | bytes 6291460
  6.5 57.3 %all-gather.2.cloned.1.call-start = ((), (), s32[]{:S(2)}) async-start(), calls=%async_computation.2 | async-start | bytes 5242880 | tf_op jit(solution)/shard_map/all_gather | solution.py:19
  73.9 1.7 copy-start.1
  83.2 102.5 %all-to-all-start = ((bf16[32,1,4,128,128]{4,3,2,1,0:T(8,128)(2,1)}), bf16[32,1,4,128,128]{4,3,2,1,0:T(8,128)(2,1)}, u32[]{:S(2)}, u32[]{:S(2)}) async-start(bf16[32,1,4,128,128]{4,3,2,1,0:T(8,128)(2,1)} %stack.2), calls=%async_computation | async-start | bytes 8388608 | tf_op jit(solution)/shard_map/all_to_all | solution.py:9
  92.9 157.6 %reduce-scatter.2.cloned.1.call-start = ((), (), s32[]{:S(2)}) async-start(), calls=%async_computation.3 | async-start | bytes 5242880 | tf_op jit(solution)/shard_map/reduce_scatter | solution.py:52
  97.4 6.3 %copy-start.4 = (bf16[64,4,8,128]{3,2,1,0:T(8,128)(2,1)}, bf16[64,4,8,128]{3,2,1,0:T(8,128)(2,1)S(1)}, u32[]{:S(2)}) copy-start(bf16[64,4,8,128]{3,2,1,0:T(8,128)(2,1)S(1)} %get-tuple-element.6) | copy-start | bytes 1572868
  103.7 85.4 %copy-start.7 = (f32[4,128,128]{2,1,0:T(8,128)S(1)}, f32[4,128,128]{2,1,0:T(8,128)}, u32[]{:S(2)}) copy-start(f32[4,128,128]{2,1,0:T(8,128)} %param.7) | copy-start | bytes 786436
  185.7 3.4 %copy-start.5 = (bf16[64,4,8,128]{3,2,1,0:T(8,128)(2,1)S(1)}, bf16[64,4,8,128]{3,2,1,0:T(8,128)(2,1)}, u32[]{:S(2)}) copy-start(bf16[64,4,8,128]{3,2,1,0:T(8,128)(2,1)} %copy-done.4) | copy-start | bytes 1572868
  185.7 3.4 %copy-start.6 = (f32[4,128,512]{2,1,0:T(8,128)S(1)}, f32[4,128,512]{2,1,0:T(8,128)}, u32[]{:S(2)}) copy-start(f32[4,128,512]{2,1,0:T(8,128)} %fusion.1) | copy-start | bytes 3145732
  185.7 3.8 %copy-start.3 = (bf16[64,4,8,128]{3,2,1,0:T(8,128)(2,1)S(1)}, bf16[64,4,8,128]{3,2,1,0:T(8,128)(2,1)}, u32[]{:S(2)}) copy-start(bf16[64,4,8,128]{3,2,1,0:T(8,128)(2,1)} %get-tuple-element.7) | copy-start | bytes 1572868
  200.7 49.8 %copy-start.2 = (bf16[256,2048]{1,0:T(8,128)(2,1)S(1)}, bf16[256,2048]{1,0:T(8,128)(2,1)}, u32[]{:S(2)}) copy-start(bf16[256,2048]{1,0:T(8,128)(2,1)} %param.4) | copy-start | bytes 3145732
Sparse Core Ops, SparseCore 0:
  9.2 54.5 all-gather.1
  200.8 49.5 reduce-scatter.1
